TPU v7x, 32 devices: a whole 2x2x4 slice. The times are simulated.
32 devices in a mesh: dp: 8 (over z, x), seq: 4 (over y, core).
Axes of the slice: x: 2, y: 2, z: 4, core: 2. Of those that a mesh axis runs over, the one named last changes fastest.
Arguments:
- queries: bfloat16 [8, 512, 2048], P('dp', 'seq'), may hold values from -72 to 72
- hit_keys: bfloat16 [8, 512, 2048], P('dp', 'seq'), may hold values from -12 to 12
- hit_values: bfloat16 [8, 512, 2048], P('dp', 'seq'), may hold values from -6 to 6
- hit_counts: int32 [8], P('dp'), may hold values from 128 to 512, as said below
- master_weight: float32 [8, 256, 2048], P('dp', None, 'seq'), may hold values from -0.5 to 0.5
- first_moment: float32 [8, 256, 2048], P('dp', None, 'seq'), may hold values from -4 to 4
- second_moment: float32 [8, 256, 2048], P('dp', None, 'seq'), may hold values from 0.1 to 4
- gradient: float32 [8, 256, 2048], P('dp', None, 'seq'), may hold values from -6 to 6
- owner_bucket: int32 [8], replicated, may hold values from 0 to 7, each once
Outputs:
- projected: bfloat16 [8, 512, 2048], P('dp', 'seq')
- new_master: float32 [8, 256, 2048], P('dp', None, 'seq')
- new_first: float32 [8, 256, 2048], P('dp', None, 'seq')
- new_second: float32 [8, 256, 2048], P('dp', None, 'seq')
Inputs may be any that keep to these rules, and one draw needn't show every extreme that they name: The valid hits of event e are its first hit_counts[e] slots; some event is full. `owner_bucket`: each bucket is held by exactly one owner.
All inputs are finite; a program needn't handle non-finite values.
Results may differ from a plain program's by a relative error of at most 0.0063.
Values may be sent and summed in bfloat16 or wider, within the bound.
No kernel may reach another device: no remote copies, remote signals or barrier semaphores. Data moves between devices by JAX's collectives and lax.ppermute only.
A program may use at most 64 MiB of HBM per device.

v0:
```python
import jax
import jax.numpy as jnp
from jax import lax
from jax.sharding import PartitionSpec as P

HEAD_DIM = 128
beta_one = 0.9
beta_two = 0.999
learn_rate = 0.003
weight_decay = 0.1
epsilon = 1e-08
step_count = 10.0
block_rows = 512


def adam_update(master_weight, first_moment, second_moment, gradient):
    new_first = beta_one * first_moment + (1.0 - beta_one) * gradient
    new_second = beta_two * second_moment + (1.0 - beta_two) * gradient * gradient
    first_hat = new_first / (1.0 - beta_one**step_count)
    second_hat = new_second / (1.0 - beta_two**step_count)
    new_master = master_weight - learn_rate * (
        first_hat / (jnp.sqrt(second_hat) + epsilon) + weight_decay * master_weight
    )
    return (new_master, new_first, new_second)


def attend_head(head_query, head_keys, head_values, count):
    length = head_query.shape[0]
    block = min(block_rows, length)
    scale = head_query.shape[1] ** (-0.5)
    valid = lax.broadcasted_iota(jnp.int32, (1, length), 1) < count

    def one_block(rows):
        scores = (
            lax.dot_general(
                rows, head_keys, (((1,), (1,)), ((), ())), preferred_element_type=jnp.float32
            )
            * scale
        )
        scores = jnp.where(valid, scores, -jnp.inf)
        top = jnp.max(scores, axis=1, keepdims=True)
        expo = jnp.exp(scores - top)
        weights = (expo / jnp.sum(expo, axis=1, keepdims=True)).astype(jnp.bfloat16)
        return jnp.dot(weights, head_values, preferred_element_type=jnp.float32).astype(
            jnp.bfloat16
        )

    blocks = head_query.reshape(length // block, block, head_query.shape[1])
    return lax.map(one_block, blocks).reshape(length, head_query.shape[1])


def body(
    queries,
    hit_keys,
    hit_values,
    hit_counts,
    master_weight,
    first_moment,
    second_moment,
    gradient,
    owner_bucket,
):
    new_master, new_first, new_second = adam_update(
        master_weight, first_moment, second_moment, gradient
    )
    weight_half = new_master.astype(jnp.bfloat16)
    groups = lax.axis_size("seq")
    owners = lax.axis_size("dp")
    tok_rows = queries.shape[1]
    width = queries.shape[2]
    per_group = width // groups
    heads_here = per_group // HEAD_DIM
    count = hit_counts[0]
    matches = owner_bucket[:, None] == jnp.arange(owners, dtype=jnp.int32)[None, :]
    inverse = jnp.sum(jnp.where(matches, jnp.arange(owners, dtype=jnp.int32)[:, None], 0), axis=0)

    def split_heads(array):
        return array.reshape(1, tok_rows, groups, heads_here, HEAD_DIM)

    query_part = lax.all_to_all(
        split_heads(queries), "seq", split_axis=2, concat_axis=1, tiled=True
    )
    keys_part = lax.all_to_all(
        split_heads(hit_keys), "seq", split_axis=2, concat_axis=1, tiled=True
    )
    values_part = lax.all_to_all(
        split_heads(hit_values), "seq", split_axis=2, concat_axis=1, tiled=True
    )
    n_heads = query_part.shape[3]

    def one_head(index):
        head_query = lax.dynamic_index_in_dim(query_part, index, 3, keepdims=False)[0, :, 0, :]
        head_keys = lax.dynamic_index_in_dim(keys_part, index, 3, keepdims=False)[0, :, 0, :]
        head_values = lax.dynamic_index_in_dim(values_part, index, 3, keepdims=False)[0, :, 0, :]
        return attend_head(head_query, head_keys, head_values, count)

    outputs = lax.map(one_head, jnp.arange(n_heads, dtype=jnp.int32))
    attended = jnp.moveaxis(outputs, 0, 1)[None, :, None, :, :]
    returned = lax.all_to_all(attended, "seq", split_axis=1, concat_axis=2, tiled=True)
    rows_in = returned.reshape(tok_rows, width)
    owned = lax.all_gather(weight_half, "dp", axis=0, tiled=True)
    full = lax.all_gather(owned, "seq", axis=2, tiled=True)
    projection = jnp.take(full, inverse, axis=0).reshape(width, width)
    total = jnp.dot(rows_in, projection, preferred_element_type=jnp.float32)
    projected = total.astype(jnp.bfloat16)[None]
    return (projected, new_master, new_first, new_second)


def solution(mesh):
    return jax.shard_map(
        body,
        mesh=mesh,
        in_specs=(
            P("dp", "seq", None),
            P("dp", "seq", None),
            P("dp", "seq", None),
            P("dp"),
            P("dp", None, "seq"),
            P("dp", None, "seq"),
            P("dp", None, "seq"),
            P("dp", None, "seq"),
            P(),
        ),
        out_specs=(
            P("dp", "seq", None),
            P("dp", None, "seq"),
            P("dp", None, "seq"),
            P("dp", None, "seq"),
        ),
        check_vma=False,
    )
```

profile of v0, /device:TPU:0, one launch (start us, length us, event | category | flops | bytes accessed | tf_op | source)
XLA Modules:
  0.0 175.6 jit_solution(9775890406966182870)
XLA Ops:
  7.2 0.0 copy-start
  7.2 0.0 copy-start.1
  7.2 0.0 copy-start.2
  7.2 0.0 all-gather.3.cloned.1.call-start
  7.2 3.1 %fusion.15 = (bf16[1,256,512]{2,1,0:T(8,128)(2,1)}, f32[1,256,512]{2,1,0:T(8,128)}, f32[1,256,512]{2,1,0:T(8,128)}, f32[1,256,512]{2,1,0:T(8,128)}) fusion(f32[1,256,512]{2,1,0:T(8,128)} %param.15, f32[1,256,512]{2,1,0:T(8,128)} %param.18, f32[1,256,512]{2,1,0:T(8,128)} %param.16, f32[1,256,512]{2,1,0:T(8,128)} %param.17), kind=kLoop, calls=%fused_computation.33 | loop fusion | flops 2097152 | bytes 3932160 | tf_op jit(solution)/shard_map/convert_element_type | solution.py:66
  10.3 0.0 all-gather.3.cloned.1.call-update
  10.4 0.0 all-gather.5.cloned.1.call-start
  10.4 52.3 %all-gather.3.cloned.1.call-done = bf16[8,256,512]{2,1,0:T(8,128)(2,1)} async-done(((bf16[1,256,512]{2,1,0:T(8,128)(2,1)}), bf16[8,256,512]{2,1,0:T(8,128)(2,1)}) %all-gather.3.cloned.1.call-update) | async-done | bytes 2097168 | tf_op jit(solution)/shard_map/all_gather | solution.py:101
  62.7 0.0 all-gather.5.cloned.1.call-update
  62.8 1.3 copy.41
  64.1 1.0 copy.42
  65.1 3.5 %all-to-all-start.1 = ((bf16[1,128,4,4,128]{4,1,3,0,2:T(8,128)(2,1)}), bf16[1,128,4,4,128]{4,1,3,0,2:T(8,128)(2,1)S(1)}, u32[]{:S(2)}, u32[]{:S(2)}) async-start(bf16[1,128,4,4,128]{4,1,3,0,2:T(8,128)(2,1)} %copy.42), calls=%async_computation.1 | async-start | bytes 1048576 | tf_op jit(solution)/shard_map/all_to_all | solution.py:83
  68.6 0.0 copy-done
  68.6 0.3 copy.44
  68.9 1.0 copy.45
  69.9 10.8 %all-to-all-done.1 = bf16[1,128,4,4,128]{4,1,3,0,2:T(8,128)(2,1)S(1)} async-done(((bf16[1,128,4,4,128]{4,1,3,0,2:T(8,128)(2,1)}), bf16[1,128,4,4,128]{4,1,3,0,2:T(8,128)(2,1)S(1)}, u32[]{:S(2)}, u32[]{:S(2)}) %all-to-all-start.1) | async-done | bytes 524320 | tf_op jit(solution)/shard_map/all_to_all | solution.py:83
  80.7 3.5 %all-to-all-start.2 = ((bf16[1,128,4,4,128]{4,1,3,0,2:T(8,128)(2,1)}), bf16[1,128,4,4,128]{4,1,3,0,2:T(8,128)(2,1)S(1)}, u32[]{:S(2)}, u32[]{:S(2)}) async-start(bf16[1,128,4,4,128]{4,1,3,0,2:T(8,128)(2,1)} %copy.45), calls=%async_computation.2 | async-start | bytes 1048576 | tf_op jit(solution)/shard_map/all_to_all | solution.py:86
  84.2 0.0 copy-done.1
  84.2 0.3 copy.38
  84.5 1.0 copy.39
  85.5 13.4 %all-to-all-done.2 = bf16[1,128,4,4,128]{4,1,3,0,2:T(8,128)(2,1)S(1)} async-done(((bf16[1,128,4,4,128]{4,1,3,0,2:T(8,128)(2,1)}), bf16[1,128,4,4,128]{4,1,3,0,2:T(8,128)(2,1)S(1)}, u32[]{:S(2)}, u32[]{:S(2)}) %all-to-all-start.2) | async-done | bytes 524320 | tf_op jit(solution)/shard_map/all_to_all | solution.py:86
  99.0 3.5 %all-to-all-start = ((bf16[1,128,4,4,128]{4,1,3,0,2:T(8,128)(2,1)}), bf16[1,128,4,4,128]{4,1,3,0,2:T(8,128)(2,1)S(1)}, u32[]{:S(2)}, u32[]{:S(2)}) async-start(bf16[1,128,4,4,128]{4,1,3,0,2:T(8,128)(2,1)} %copy.39), calls=%async_computation | async-start | bytes 1048576 | tf_op jit(solution)/shard_map/all_to_all | solution.py:80
  102.4 0.0 copy-done.2
  102.5 0.1 select_reduce_fusion
  102.6 14.5 %all-to-all-done = bf16[1,128,4,4,128]{4,1,3,0,2:T(8,128)(2,1)S(1)} async-done(((bf16[1,128,4,4,128]{4,1,3,0,2:T(8,128)(2,1)}), bf16[1,128,4,4,128]{4,1,3,0,2:T(8,128)(2,1)S(1)}, u32[]{:S(2)}, u32[]{:S(2)}) %all-to-all-start) | async-done | bytes 524320 | tf_op jit(solution)/shard_map/all_to_all | solution.py:80
  117.2 16.6 %while.10 = (s32[]{:T(128)}, bf16[4,512,128]{2,1,0:T(8,128)(2,1)S(1)}, s32[]{:T(128)}, s32[4]{0:T(128)S(1)}, bf16[1,512,1,4,128]{4,1,3,2,0:T(8,128)(2,1)S(1)}, /...) while((s32[]{:T(128)}, ...), condition=%wide.region_3.4_spmd, body=%wide.region_0.3_spmd.sunk | while | flops 136379904 | bytes 3682463 | solution.py:97
  117.3 0.6 dynamic_slice.40
  119.8 0.7 iota_compare_fusion.3
  120.4 0.3 fusion.25
  120.8 0.2 fusion.26
  121.0 0.4 fusion.27
  121.4 0.6 dynamic_slice.40
  123.9 0.7 iota_compare_fusion.3
  124.6 0.3 fusion.25
  124.9 0.2 fusion.26
  125.1 0.4 fusion.27
  125.6 0.6 dynamic_slice.40
  128.1 0.7 iota_compare_fusion.3
  128.8 0.3 fusion.25
  129.1 0.2 fusion.26
  129.3 0.4 fusion.27
  129.7 0.6 dynamic_slice.40
  132.3 0.7 iota_compare_fusion.3
  132.9 0.3 fusion.25
  133.2 0.2 fusion.26
  133.4 0.4 fusion.27
  133.9 1.2 copy.51
  135.1 3.5 %all-to-all-start.3 = ((bf16[1,512,1,4,128]{4,3,2,0,1:T(4,128)(2,1)}), bf16[1,512,1,4,128]{4,3,2,0,1:T(4,128)(2,1)S(1)}, u32[]{:S(2)}, u32[]{:S(2)}) async-start(bf16[1,512,1,4,128]{4,3,2,0,1:T(4,128)(2,1)} %bitcast.54), calls=%async_computation.3 | async-start | bytes 1048576 | tf_op jit(solution)/shard_map/all_to_all | solution.py:99
  138.6 8.8 %all-to-all-done.3 = bf16[1,512,1,4,128]{4,3,2,0,1:T(4,128)(2,1)S(1)} async-done(((bf16[1,512,1,4,128]{4,3,2,0,1:T(4,128)(2,1)}), bf16[1,512,1,4,128]{4,3,2,0,1:T(4,128)(2,1)S(1)}, u32[]{:S(2)}, u32[]{:S(2)}) %all-to-all-start.3) | async-done | bytes 524320 | tf_op jit(solution)/shard_map/all_to_all | solution.py:99
  147.4 0.1 copy.48
  147.4 0.3 copy.49
  147.7 0.0 all-gather.5.cloned.1.call-done
  147.8 8.1 %gather_fusion = bf16[8,256,2048]{2,1,0:T(8,128)(2,1)} fusion(bf16[8,256,2048]{2,1,0:T(8,128)(2,1)} %all-gather.5.cloned.1.call-done, s32[1024]{0:T(1024)S(1)} %pad_clamp_fusion), kind=kCustom, calls=%fused_computation | custom fusion | bytes 16777248 | tf_op jit(solution)/shard_map/jit(_take)/gather | solution.py:103
  155.8 7.5 %broadcast_select_fusion = bf16[8,256,2048]{2,1,0:T(8,128)(2,1)} fusion(bf16[8,256,2048]{2,1,0:T(8,128)(2,1)} %gather_fusion, pred[8]{0:T(512)(128)(4,1)S(1)} %compare_and_fusion), kind=kLoop, calls=%fused_computation.18 | loop fusion | flops 4194304 | bytes 16777224 | tf_op jit(solution)/shard_map/jit(_take)/select_n | solution.py:103
  163.3 5.5 %fusion.12 = bf16[1,128,2048]{2,1,0:T(8,128)(2,1)} fusion(bf16[128,2048]{0,1:T(8,128)(2,1)S(1)} %bitcast.66, bf16[2048,2048]{1,0:T(8,128)(2,1)} %bitcast.65), kind=kOutput, calls=%fused_computation.20 | convolution fusion | flops 1074003968 | bytes 9437184 | tf_op jit(solution)/shard_map/dot_general | solution.py:104
  (8 shorter events, 0.1 us)
Async XLA Ops:
  7.2 61.4 %copy-start = (bf16[1,128,2048]{2,1,0:T(8,128)(2,1)S(1)}, bf16[1,128,2048]{2,1,0:T(8,128)(2,1)}, u32[]{:S(2)}) copy-start(bf16[1,128,2048]{2,1,0:T(8,128)(2,1)} %param.13) | copy-start | bytes 1572868
  7.2 77.0 %copy-start.1 = (bf16[1,128,2048]{2,1,0:T(8,128)(2,1)S(1)}, bf16[1,128,2048]{2,1,0:T(8,128)(2,1)}, u32[]{:S(2)}) copy-start(bf16[1,128,2048]{2,1,0:T(8,128)(2,1)} %param.11) | copy-start | bytes 1572868
  7.2 95.3 %copy-start.2 = (s32[8]{0:T(128)S(1)}, s32[8]{0:T(128)}, u32[]{:S(2)}) copy-start(s32[8]{0:T(128)} %param.19) | copy-start | bytes 100
  7.2 55.6 %all-gather.3.cloned.1.call-start = ((), (), s32[]{:S(2)}) async-start(), calls=%async_computation.4 | async-start | bytes 2359296 | tf_op jit(solution)/shard_map/all_gather | solution.py:101
  10.4 137.4 %all-gather.5.cloned.1.call-start = ((), (), s32[]{:S(2)}) async-start(), calls=%async_computation.5 | async-start | bytes 10485760 | tf_op jit(solution)/shard_map/all_gather | solution.py:102
  65.1 15.6 %all-to-all-start.1 = ((bf16[1,128,4,4,128]{4,1,3,0,2:T(8,128)(2,1)}), bf16[1,128,4,4,128]{4,1,3,0,2:T(8,128)(2,1)S(1)}, u32[]{:S(2)}, u32[]{:S(2)}) async-start(bf16[1,128,4,4,128]{4,1,3,0,2:T(8,128)(2,1)} %copy.42), calls=%async_computation.1 | async-start | bytes 1048576 | tf_op jit(solution)/shard_map/all_to_all | solution.py:83
  80.7 18.2 %all-to-all-start.2 = ((bf16[1,128,4,4,128]{4,1,3,0,2:T(8,128)(2,1)}), bf16[1,128,4,4,128]{4,1,3,0,2:T(8,128)(2,1)S(1)}, u32[]{:S(2)}, u32[]{:S(2)}) async-start(bf16[1,128,4,4,128]{4,1,3,0,2:T(8,128)(2,1)} %copy.45), calls=%async_computation.2 | async-start | bytes 1048576 | tf_op jit(solution)/shard_map/all_to_all | solution.py:86
  99.0 18.2 %all-to-all-start = ((bf16[1,128,4,4,128]{4,1,3,0,2:T(8,128)(2,1)}), bf16[1,128,4,4,128]{4,1,3,0,2:T(8,128)(2,1)S(1)}, u32[]{:S(2)}, u32[]{:S(2)}) async-start(bf16[1,128,4,4,128]{4,1,3,0,2:T(8,128)(2,1)} %copy.39), calls=%async_computation | async-start | bytes 1048576 | tf_op jit(solution)/shard_map/all_to_all | solution.py:80
  135.1 12.3 %all-to-all-start.3 = ((bf16[1,512,1,4,128]{4,3,2,0,1:T(4,128)(2,1)}), bf16[1,512,1,4,128]{4,3,2,0,1:T(4,128)(2,1)S(1)}, u32[]{:S(2)}, u32[]{:S(2)}) async-start(bf16[1,512,1,4,128]{4,3,2,0,1:T(4,128)(2,1)} %bitcast.54), calls=%async_computation.3 | async-start | bytes 1048576 | tf_op jit(solution)/shard_map/all_to_all | solution.py:99
Sparse Core Ops, SparseCore 0:
  10.7 51.9 all-gather.2
  64.3 71.0 all-gather.4
where the time goes:
time: 176 us
  waiting for transfers between devices  100 us (57%)
  local copies, waits for them, and re-layouts  17 us (10%)
  between operations  14.2 us (8%)
  other arithmetic  14.1 us (8%)
  starting transfers between devices  14 us (8%)
  matrix products  8.47 us (5%)
  loops' own time  7.88 us (4%)
    all_gather x1, waiting for transfers between devices, body(): owned = lax.all_gather(weight_half, 'dp', axis=0, tiled=True)  52.3 us
    all_to_all x1, waiting for transfers between devices, body(): lax.all_to_all(split_heads(queries), 'seq', split_axis=2, concat_axis=1,...  14.5 us
    all_to_all x1, waiting for transfers between devices, body(): lax.all_to_all(split_heads(hit_values), 'seq', split_axis=2, concat_axis=...  13.4 us
    all_to_all x1, waiting for transfers between devices, body(): lax.all_to_all(split_heads(hit_keys), 'seq', split_axis=2, concat_axis=1,...  10.8 us
    all_to_all x1, waiting for transfers between devices, body(): lax.all_to_all(attended, 'seq', split_axis=1, concat_axis=2, tiled=True)  8.77 us
    gather x1, local copies, waits for them, and re-layouts, body(): projection = jnp.take(full, inverse, axis=0).reshape(width, width)  8.08 us
    another operation x1, loops' own time, body(): outputs = lax.map(one_head, jnp.arange(n_heads, dtype=jnp.int32))  7.88 us
    select_n x2, other arithmetic, body(): projection = jnp.take(full, inverse, axis=0).reshape(width, width)  7.49 us
  transfers between devices with their start and end apart: 6, of which 5 were waited for; matrix products, arithmetic and copies ran while one was open for 9% of the time, Pallas kernels for 0%

commit v1 on v0

--- a/solution.py
+++ b/solution.py
@@ -11,6 +11,30 @@
 epsilon = 1e-08
 step_count = 10.0
 block_rows = 512
+
+
+def cut_along(x, dim, peers):
+    dims = x.shape
+    blocks = x.reshape(*dims[:dim], peers, dims[dim] // peers, *dims[dim + 1 :])
+    return jnp.moveaxis(blocks, dim, 0)
+
+
+def laid_out(parts, dim):
+    parts = jnp.moveaxis(parts, 0, dim)
+    shape = parts.shape
+    return parts.reshape(*shape[:dim], shape[dim] * shape[dim + 1], *shape[dim + 2 :])
+
+
+def exchange_directly(x, axis, split_dim, concat_dim):
+    devices, here = (lax.axis_size(axis), lax.axis_index(axis))
+    blocks = cut_along(x, split_dim, devices)
+    filled = blocks
+    for lap in range(1, devices):
+        target, source = ((here + lap) % devices, (here - lap) % devices)
+        sent = lax.dynamic_index_in_dim(blocks, target, 0)
+        received = lax.ppermute(sent, axis, [(i, (i + lap) % devices) for i in range(devices)])
+        filled = lax.dynamic_update_slice_in_dim(filled, received, source, axis=0)
+    return laid_out(filled, concat_dim)
 
 
 def adam_update(master_weight, first_moment, second_moment, gradient):
@@ -77,9 +101,7 @@
     def split_heads(array):
         return array.reshape(1, tok_rows, groups, heads_here, HEAD_DIM)
 
-    query_part = lax.all_to_all(
-        split_heads(queries), "seq", split_axis=2, concat_axis=1, tiled=True
-    )
+    query_part = exchange_directly(split_heads(queries), "seq", 2, 1)
     keys_part = lax.all_to_all(
         split_heads(hit_keys), "seq", split_axis=2, concat_axis=1, tiled=True
     )

time: 176 us -> 169 us (0.960)
  waiting for transfers between devices: 100 us -> 94.6 us
    all_to_all x1 -> x0, waiting for transfers between devices: 14.5 us -> none  [body(): lax.all_to_all(split_heads(queries), 'seq', split_axis=2, concat_axis=1,...]
    all_to_all x1, waiting for transfers between devices: 8.77 us -> 14.7 us  [body(): lax.all_to_all(attended, 'seq', split_axis=1, concat_axis=2, tiled=True)]
    ppermute x0 -> x3, waiting for transfers between devices: none -> 4.84 us  [exchange_directly(): lax.ppermute(sent, axis, [(i, (i + lap) % devices) for i in range(devices)])]
    all_to_all x1, waiting for transfers between devices: 10.8 us -> 7.08 us  [body(): lax.all_to_all(split_heads(hit_keys), 'seq', split_axis=2, concat_axis=1,...]
    ppermute x0 -> x3, starting transfers between devices: none -> 3.57 us  [exchange_directly(): lax.ppermute(sent, axis, [(i, (i + lap) % devices) for i in range(devices)])]
    all_to_all x1 -> x0, starting transfers between devices: 3.47 us -> none  [body(): lax.all_to_all(split_heads(queries), 'seq', split_axis=2, concat_axis=1,...]
    all_gather x1, waiting for transfers between devices: 0.02 us -> 2.36 us  [body(): full = lax.all_gather(owned, 'seq', axis=2, tiled=True)]
  transfers between devices with their start and end apart: 6 -> 8, of which waited for: 5 -> 7; matrix products, arithmetic and copies ran while one was open for 9% -> 9% of each run, Pallas kernels for 0% -> 0%
where the time goes in v1:
time: 169 us
  waiting for transfers between devices  94.6 us (56%)
  local copies, waits for them, and re-layouts  16.4 us (10%)
  between operations  14.3 us (8%)
  starting transfers between devices  14.1 us (8%)
  other arithmetic  14.1 us (8%)
  matrix products  8.46 us (5%)
  loops' own time  6.83 us (4%)
    all_gather x1, waiting for transfers between devices, body(): owned = lax.all_gather(weight_half, 'dp', axis=0, tiled=True)  52.3 us
    all_to_all x1, waiting for transfers between devices, body(): lax.all_to_all(attended, 'seq', split_axis=1, concat_axis=2, tiled=True)  14.7 us
    all_to_all x1, waiting for transfers between devices, body(): lax.all_to_all(split_heads(hit_values), 'seq', split_axis=2, concat_axis=...  13.3 us
    gather x1, local copies, waits for them, and re-layouts, body(): projection = jnp.take(full, inverse, axis=0).reshape(width, width)  8.06 us
    select_n x2, other arithmetic, body(): projection = jnp.take(full, inverse, axis=0).reshape(width, width)  7.48 us
    all_to_all x1, waiting for transfers between devices, body(): lax.all_to_all(split_heads(hit_keys), 'seq', split_axis=2, concat_axis=1,...  7.08 us
    another operation x1, loops' own time, body(): outputs = lax.map(one_head, jnp.arange(n_heads, dtype=jnp.int32))  6.83 us
    dot_general x1, matrix products, body(): total = jnp.dot(rows_in, projection, preferred_element_type=jnp.float32)  5.46 us
  transfers between devices with their start and end apart: 8, of which 7 were waited for; matrix products, arithmetic and copies ran while one was open for 9% of the time, Pallas kernels for 0%

profile of v1, /device:TPU:0, one launch (start us, length us, event | category | flops | bytes accessed | tf_op | source)
XLA Modules:
  0.0 168.8 jit_solution(5370804993864776043)
XLA Ops:
  7.2 0.0 copy-start
  7.2 0.0 copy-start.1
  7.2 0.0 copy-start.2
  7.2 0.0 all-gather.3.cloned.1.call-start
  7.2 3.1 %fusion.15 = (bf16[1,256,512]{2,1,0:T(8,128)(2,1)}, f32[1,256,512]{2,1,0:T(8,128)}, f32[1,256,512]{2,1,0:T(8,128)}, f32[1,256,512]{2,1,0:T(8,128)}) fusion(f32[1,256,512]{2,1,0:T(8,128)} %param.15, f32[1,256,512]{2,1,0:T(8,128)} %param.18, f32[1,256,512]{2,1,0:T(8,128)} %param.16, f32[1,256,512]{2,1,0:T(8,128)} %param.17), kind=kLoop, calls=%fused_computation.43 | loop fusion | flops 2097152 | bytes 3932160 | tf_op jit(solution)/shard_map/convert_element_type | solution.py:90
  10.3 0.0 all-gather.3.cloned.1.call-update
  10.4 0.0 all-gather.5.cloned.1.call-start
  10.4 52.3 %all-gather.3.cloned.1.call-done = bf16[8,256,512]{2,1,0:T(8,128)(2,1)} async-done(((bf16[1,256,512]{2,1,0:T(8,128)(2,1)}), bf16[8,256,512]{2,1,0:T(8,128)(2,1)}) %all-gather.3.cloned.1.call-update) | async-done | bytes 2097168 | tf_op jit(solution)/shard_map/all_gather | solution.py:123
  62.7 0.0 all-gather.5.cloned.1.call-update
  62.8 1.3 copy.53
  64.1 1.0 copy.54
  65.1 3.5 %all-to-all-start = ((bf16[1,128,4,4,128]{4,1,3,0,2:T(8,128)(2,1)}), bf16[1,128,4,4,128]{4,1,3,0,2:T(8,128)(2,1)S(1)}, u32[]{:S(2)}, u32[]{:S(2)}) async-start(bf16[1,128,4,4,128]{4,1,3,0,2:T(8,128)(2,1)} %copy.54), calls=%async_computation | async-start | bytes 1048576 | tf_op jit(solution)/shard_map/all_to_all | solution.py:105
  68.6 0.0 copy-done
  68.6 0.4 reshape_reshape.3
  69.0 0.1 constant_dynamic-slice_fusion
  69.2 0.5 collective-permute-start
  69.7 1.7 %collective-permute-start.1 = (bf16[1,1,128,1,4,128]{5,2,0,4,3,1:T(8,128)(2,1)S(1)}, bf16[1,1,128,1,4,128]{5,2,0,4,3,1:T(8,128)(2,1)S(1)}, u32[]{:S(2)}, u32[]{:S(2)}) collective-permute-start(bf16[1,1,128,1,4,128]{5,2,0,4,3,1:T(8,128)(2,1)S(1)} %bitcast.82), channel_id=1, source_target_pairs={{0,2},{1,3},{2,0},{3,1},{4,6},{5,7},{6,4},{7,5},{8,10},{9,11},{10,... | collective-permute-start | bytes 393224 | tf_op jit(solution)/shard_map/ppermute | solution.py:35
  71.5 1.4 collective-permute-start.2
  72.8 0.0 copy-done.1
  72.8 0.3 copy.56
  73.1 1.0 copy.57
  74.1 7.1 %all-to-all-done = bf16[1,128,4,4,128]{4,1,3,0,2:T(8,128)(2,1)S(1)} async-done(((bf16[1,128,4,4,128]{4,1,3,0,2:T(8,128)(2,1)}), bf16[1,128,4,4,128]{4,1,3,0,2:T(8,128)(2,1)S(1)}, u32[]{:S(2)}, u32[]{:S(2)}) %all-to-all-start) | async-done | bytes 524320 | tf_op jit(solution)/shard_map/all_to_all | solution.py:105
  81.2 3.5 %all-to-all-start.1 = ((bf16[1,128,4,4,128]{4,1,3,0,2:T(8,128)(2,1)}), bf16[1,128,4,4,128]{4,1,3,0,2:T(8,128)(2,1)S(1)}, u32[]{:S(2)}, u32[]{:S(2)}) async-start(bf16[1,128,4,4,128]{4,1,3,0,2:T(8,128)(2,1)} %copy.57), calls=%async_computation.1 | async-start | bytes 1048576 | tf_op jit(solution)/shard_map/all_to_all | solution.py:108
  84.7 0.0 copy-done.2
  84.7 0.1 select_reduce_fusion
  84.8 0.1 copy.68
  84.9 0.0 collective-permute-done
  85.0 1.8 %collective-permute-done.1 = bf16[1,1,128,1,4,128]{5,2,0,4,3,1:T(8,128)(2,1)S(1)} collective-permute-done((bf16[1,1,128,1,4,128]{5,2,0,4,3,1:T(8,128)(2,1)S(1)}, bf16[1,1,128,1,4,128]{5,2,0,4,3,1:T(8,128)(2,1)S(1)}, u32[]{:S(2)}, u32[]{:S(2)}) %collective-permute-start.1) | collective-permute-done | bytes 131104 | tf_op jit(solution)/shard_map/ppermute | solution.py:35
  86.8 3.0 %collective-permute-done.2 = bf16[1,1,128,1,4,128]{5,2,0,4,3,1:T(8,128)(2,1)S(1)} collective-permute-done((bf16[1,1,128,1,4,128]{5,2,0,4,3,1:T(8,128)(2,1)S(1)}, bf16[1,1,128,1,4,128]{5,2,0,4,3,1:T(8,128)(2,1)S(1)}, u32[]{:S(2)}, u32[]{:S(2)}) %collective-permute-start.2) | collective-permute-done | bytes 131104 | tf_op jit(solution)/shard_map/ppermute | solution.py:35
  89.9 13.3 %all-to-all-done.1 = bf16[1,128,4,4,128]{4,1,3,0,2:T(8,128)(2,1)S(1)} async-done(((bf16[1,128,4,4,128]{4,1,3,0,2:T(8,128)(2,1)}), bf16[1,128,4,4,128]{4,1,3,0,2:T(8,128)(2,1)S(1)}, u32[]{:S(2)}, u32[]{:S(2)}) %all-to-all-start.1) | async-done | bytes 524320 | tf_op jit(solution)/shard_map/all_to_all | solution.py:108
  103.3 15.6 %while.10 = (s32[]{:T(128)}, bf16[4,512,128]{2,1,0:T(8,128)(2,1)S(1)}, s32[]{:T(128)}, s32[4]{0:T(128)S(1)}, bf16[1,512,1,4,128]{4,1,3,2,0:T(8,128)(2,1)S(1)}, /...) while((s32[]{:T(128)}, ...), condition=%wide.region_3.4_spmd, body=%wide.region_0.3_spmd.sunk | while | flops 136379904 | bytes 3682471 | solution.py:119
  103.3 0.6 dynamic_slice.53
  105.5 0.7 iota_compare_fusion.3
  106.2 0.3 fusion.25
  106.5 0.2 fusion.26
  106.7 0.4 fusion.27
  107.2 0.6 dynamic_slice.53
  109.4 0.7 iota_compare_fusion.3
  110.1 0.3 fusion.25
  110.4 0.2 fusion.26
  110.6 0.4 fusion.27
  111.0 0.6 dynamic_slice.53
  113.3 0.7 iota_compare_fusion.3
  114.0 0.3 fusion.25
  114.3 0.2 fusion.26
  114.5 0.4 fusion.27
  114.9 0.6 dynamic_slice.53
  117.2 0.7 iota_compare_fusion.3
  117.9 0.3 fusion.25
  118.2 0.2 fusion.26
  118.4 0.4 fusion.27
  118.8 1.2 copy.67
  120.0 3.5 %all-to-all-start.2 = ((bf16[1,512,1,4,128]{4,3,2,0,1:T(4,128)(2,1)}), bf16[1,512,1,4,128]{4,3,2,0,1:T(4,128)(2,1)S(1)}, u32[]{:S(2)}, u32[]{:S(2)}) async-start(bf16[1,512,1,4,128]{4,3,2,0,1:T(4,128)(2,1)} %bitcast.57), calls=%async_computation.2 | async-start | bytes 1048576 | tf_op jit(solution)/shard_map/all_to_all | solution.py:121
  123.5 14.7 %all-to-all-done.2 = bf16[1,512,1,4,128]{4,3,2,0,1:T(4,128)(2,1)S(1)} async-done(((bf16[1,512,1,4,128]{4,3,2,0,1:T(4,128)(2,1)}), bf16[1,512,1,4,128]{4,3,2,0,1:T(4,128)(2,1)S(1)}, u32[]{:S(2)}, u32[]{:S(2)}) %all-to-all-start.2) | async-done | bytes 524320 | tf_op jit(solution)/shard_map/all_to_all | solution.py:121
  138.3 0.1 copy.60
  138.3 0.3 copy.61
  138.6 2.4 %all-gather.5.cloned.1.call-done = bf16[8,256,2048]{2,1,0:T(8,128)(2,1)} async-done(((bf16[8,256,512]{2,1,0:T(8,128)(2,1)}), bf16[8,256,2048]{2,1,0:T(8,128)(2,1)}) %all-gather.5.cloned.1.call-update) | async-done | bytes 8388624 | tf_op jit(solution)/shard_map/all_gather | solution.py:124
  141.0 8.1 %gather_fusion = bf16[8,256,2048]{2,1,0:T(8,128)(2,1)} fusion(bf16[8,256,2048]{2,1,0:T(8,128)(2,1)} %all-gather.5.cloned.1.call-done, s32[1024]{0:T(1024)S(1)} %pad_clamp_fusion), kind=kCustom, calls=%fused_computation | custom fusion | bytes 16777248 | tf_op jit(solution)/shard_map/jit(_take)/gather | solution.py:125
  149.0 7.5 %broadcast_select_fusion = bf16[8,256,2048]{2,1,0:T(8,128)(2,1)} fusion(bf16[8,256,2048]{2,1,0:T(8,128)(2,1)} %gather_fusion, pred[8]{0:T(512)(128)(4,1)S(1)} %compare_and_fusion), kind=kLoop, calls=%fused_computation.18 | loop fusion | flops 4194304 | bytes 16777224 | tf_op jit(solution)/shard_map/jit(_take)/select_n | solution.py:125
  156.5 5.5 %fusion.12 = bf16[1,128,2048]{2,1,0:T(8,128)(2,1)} fusion(bf16[128,2048]{0,1:T(8,128)(2,1)S(1)} %bitcast.73, bf16[2048,2048]{1,0:T(8,128)(2,1)} %bitcast.72), kind=kOutput, calls=%fused_computation.20 | convolution fusion | flops 1074003968 | bytes 9437184 | tf_op jit(solution)/shard_map/dot_general | solution.py:126
  (13 shorter events, 0.2 us)
Async XLA Ops:
  7.2 61.5 %copy-start = (bf16[1,128,2048]{2,1,0:T(8,128)(2,1)S(1)}, bf16[1,128,2048]{2,1,0:T(8,128)(2,1)}, u32[]{:S(2)}) copy-start(bf16[1,128,2048]{2,1,0:T(8,128)(2,1)} %param.11) | copy-start | bytes 1572868
  7.2 65.6 %copy-start.1 = (bf16[1,128,2048]{2,1,0:T(8,128)(2,1)S(1)}, bf16[1,128,2048]{2,1,0:T(8,128)(2,1)}, u32[]{:S(2)}) copy-start(bf16[1,128,2048]{2,1,0:T(8,128)(2,1)} %param.13) | copy-start | bytes 1572868
  7.2 77.5 %copy-start.2 = (s32[8]{0:T(128)S(1)}, s32[8]{0:T(128)}, u32[]{:S(2)}) copy-start(s32[8]{0:T(128)} %param.19) | copy-start | bytes 100
  7.2 55.6 %all-gather.3.cloned.1.call-start = ((), (), s32[]{:S(2)}) async-start(), calls=%async_computation.3 | async-start | bytes 2359296 | tf_op jit(solution)/shard_map/all_gather | solution.py:123
  10.4 130.6 %all-gather.5.cloned.1.call-start = ((), (), s32[]{:S(2)}) async-start(), calls=%async_computation.4 | async-start | bytes 10485760 | tf_op jit(solution)/shard_map/all_gather | solution.py:124
  65.1 16.1 %all-to-all-start = ((bf16[1,128,4,4,128]{4,1,3,0,2:T(8,128)(2,1)}), bf16[1,128,4,4,128]{4,1,3,0,2:T(8,128)(2,1)S(1)}, u32[]{:S(2)}, u32[]{:S(2)}) async-start(bf16[1,128,4,4,128]{4,1,3,0,2:T(8,128)(2,1)} %copy.54), calls=%async_computation | async-start | bytes 1048576 | tf_op jit(solution)/shard_map/all_to_all | solution.py:105
  69.2 15.7 %collective-permute-start = (bf16[1,1,128,1,4,128]{5,2,0,4,3,1:T(8,128)(2,1)S(1)}, bf16[1,1,128,1,4,128]{5,2,0,4,3,1:T(8,128)(2,1)S(1)}, u32[]{:S(2)}, u32[]{:S(2)}) collective-permute-start(bf16[1,1,128,1,4,128]{5,2,0,4,3,1:T(8,128)(2,1)S(1)} %bitcast.83), channel_id=1, source_target_pairs={{0,1},{1,2},{2,3},{3,0},{4,5},{5,6},{6,7},{7,4},{8,9},{9,10},{10,1... | collective-permute-start | bytes 393224 | tf_op jit(solution)/shard_map/ppermute | solution.py:35
  69.7 17.1 %collective-permute-start.1 = (bf16[1,1,128,1,4,128]{5,2,0,4,3,1:T(8,128)(2,1)S(1)}, bf16[1,1,128,1,4,128]{5,2,0,4,3,1:T(8,128)(2,1)S(1)}, u32[]{:S(2)}, u32[]{:S(2)}) collective-permute-start(bf16[1,1,128,1,4,128]{5,2,0,4,3,1:T(8,128)(2,1)S(1)} %bitcast.82), channel_id=1, source_target_pairs={{0,2},{1,3},{2,0},{3,1},{4,6},{5,7},{6,4},{7,5},{8,10},{9,11},{10,... | collective-permute-start | bytes 393224 | tf_op jit(solution)/shard_map/ppermute | solution.py:35
  71.5 18.4 %collective-permute-start.2 = (bf16[1,1,128,1,4,128]{5,2,0,4,3,1:T(8,128)(2,1)S(1)}, bf16[1,1,128,1,4,128]{5,2,0,4,3,1:T(8,128)(2,1)S(1)}, u32[]{:S(2)}, u32[]{:S(2)}) collective-permute-start(bf16[1,1,128,1,4,128]{5,2,0,4,3,1:T(8,128)(2,1)S(1)} %bitcast.81), channel_id=1, source_target_pairs={{0,3},{1,0},{2,1},{3,2},{4,7},{5,4},{6,5},{7,6},{8,11},{9,8},{10,9... | collective-permute-start | bytes 393224 | tf_op jit(solution)/shard_map/ppermute | solution.py:35
  81.2 22.0 %all-to-all-start.1 = ((bf16[1,128,4,4,128]{4,1,3,0,2:T(8,128)(2,1)}), bf16[1,128,4,4,128]{4,1,3,0,2:T(8,128)(2,1)S(1)}, u32[]{:S(2)}, u32[]{:S(2)}) async-start(bf16[1,128,4,4,128]{4,1,3,0,2:T(8,128)(2,1)} %copy.57), calls=%async_computation.1 | async-start | bytes 1048576 | tf_op jit(solution)/shard_map/all_to_all | solution.py:108
  120.0 18.2 %all-to-all-start.2 = ((bf16[1,512,1,4,128]{4,3,2,0,1:T(4,128)(2,1)}), bf16[1,512,1,4,128]{4,3,2,0,1:T(4,128)(2,1)S(1)}, u32[]{:S(2)}, u32[]{:S(2)}) async-start(bf16[1,512,1,4,128]{4,3,2,0,1:T(4,128)(2,1)} %bitcast.57), calls=%async_computation.2 | async-start | bytes 1048576 | tf_op jit(solution)/shard_map/all_to_all | solution.py:121
Sparse Core Ops, SparseCore 0:
  10.7 51.9 all-gather.2
  64.3 76.6 all-gather.4
